TPU v7x, 32 devices: a whole 2x2x4 slice. The times are simulated.
32 devices in a mesh: groups: 2 (over x), ctx: 8 (over z, y), head: 2 (over core).
Axes of the slice: x: 2, y: 2, z: 4, core: 2. Of those that a mesh axis runs over, the one named last changes fastest.
Arguments:
- queries: bfloat16 [2, 256, 64, 128], P('groups', 'ctx', 'head'), parts along dimension 0, may hold values from -400 to 400
- new_keys: bfloat16 [2, 256, 8, 128], P('groups', 'ctx', 'head'), parts along dimension 0, may hold values from -5 to 5
- new_values: bfloat16 [2, 256, 8, 128], P('groups', 'ctx', 'head'), parts along dimension 0, may hold values from -6 to 6
- history_keys: bfloat16 [2, 8192, 8, 128], P('groups', 'ctx', 'head'), parts along dimension 0, may hold values from -6 to 6
- history_values: bfloat16 [2, 8192, 8, 128], P('groups', 'ctx', 'head'), parts along dimension 0, may hold values from -6 to 6
- block_mask: int32 [2, 2, 64], P('groups', None, 'ctx'), parts along dimension 0, may hold values from 0 to 1, as said below
Outputs:
- attended: bfloat16 [2, 256, 64, 128], P('groups', 'ctx', 'head'), parts along dimension 0
There are 2 independent parts, one for each index of `groups`. A program takes and returns all parts, laid end to end along the dimension named above; each array names one. Nothing has to cross between parts.
Inputs may be any that keep to these rules, and one draw needn't show every extreme that they name: `block_mask`: 0 or 1 for each pair of a block of 128 new tokens and a block of 128 history positions of the same session.
All inputs are finite; a program needn't handle non-finite values.
Results may differ from a plain program's by a relative error of at most 0.0013.
Values may be sent and summed in bfloat16 or wider, within the bound.
A program may use at most 64 MiB of HBM per device.

v0:
```python
import math

import jax
import jax.numpy as jnp
from jax import lax
from jax.sharding import PartitionSpec as P

BLK = 128


NEG = -1e30


def attend(query_rows, keys_t, values_t, visible):
    sess, rows, local_heads, head_size = query_rows.shape
    kv_local = keys_t.shape[0]
    group = local_heads // kv_local
    grouped = jnp.moveaxis(query_rows.reshape(sess, rows, kv_local, group, head_size), 2, 0)
    scale = 1.0 / math.sqrt(head_size)
    seen = visible[:, None]

    def one_head(operands):
        q_head, k_head, v_head = operands
        scores = (
            jnp.einsum("srgd,scd->sgrc", q_head, k_head, preferred_element_type=jnp.float32) * scale
        )
        masked = jnp.where(seen, scores, NEG)
        peak = jnp.max(masked, axis=-1)
        expo = jnp.where(seen, jnp.exp(masked - peak[..., None]), 0.0)
        total = jnp.sum(expo, axis=-1)
        summed = jnp.einsum(
            "sgrc,scd->sgrd", expo, v_head.astype(jnp.float32), precision=lax.Precision.HIGHEST
        )
        return (peak, total, summed)

    peak, total, summed = lax.map(one_head, (grouped, keys_t, values_t))
    peak = jnp.transpose(peak, (1, 3, 0, 2)).reshape(sess, rows, local_heads)
    total = jnp.transpose(total, (1, 3, 0, 2)).reshape(sess, rows, local_heads)
    summed = jnp.transpose(summed, (1, 3, 0, 2, 4)).reshape(sess, rows, local_heads, head_size)
    return (peak, total, summed)


def per_device(queries, new_keys, new_values, history_keys, history_values, block_mask):
    sess, own, local_heads, head_size = queries.shape
    first = lax.axis_index("ctx") * own
    qblocks = block_mask.shape[1]
    own_ids = first + lax.iota(jnp.int32, own)
    mask_float = block_mask.astype(jnp.float32)
    keys_t = jnp.moveaxis(history_keys, 2, 0)
    values_t = jnp.moveaxis(history_values, 2, 0)
    piece = lax.all_gather(queries, "ctx", axis=1, tiled=True)
    rows = piece.shape[1]
    row_ids = lax.iota(jnp.int32, rows)
    onehot = (row_ids[:, None] // BLK == lax.iota(jnp.int32, qblocks)[None, :]).astype(jnp.float32)
    live = jnp.einsum("rq,sqb->srb", onehot, mask_float)
    visible = jnp.repeat(live, BLK, axis=2) > 0.5
    peak, total, summed = attend(piece, keys_t, values_t, visible)
    peak_all = peak
    total_all = total
    summed_all = summed
    peaks, totals, sums = (
        lax.all_to_all(peak_all[None], "ctx", split_axis=2, concat_axis=0, tiled=True),
        lax.all_to_all(total_all[None], "ctx", split_axis=2, concat_axis=0, tiled=True),
        lax.all_to_all(summed_all[None], "ctx", split_axis=2, concat_axis=0, tiled=True),
    )
    hist_top = jnp.max(peaks, axis=0)
    factor = jnp.exp(peaks - hist_top[None])
    hist_total = jnp.sum(totals * factor, axis=0)
    hist_sum = jnp.sum(sums * factor[..., None], axis=0)
    key_piece = lax.all_gather(new_keys, "ctx", axis=1, tiled=True)
    value_piece = lax.all_gather(new_values, "ctx", axis=1, tiled=True)
    cols = key_piece.shape[1]
    causal = lax.iota(jnp.int32, cols)[None, :] <= own_ids[:, None]
    visible = causal[None]
    peak, total, summed = attend(
        queries, jnp.moveaxis(key_piece, 2, 0), jnp.moveaxis(value_piece, 2, 0), visible
    )
    old_peak = jnp.full((sess, own, local_heads), NEG, jnp.float32)
    top = jnp.maximum(old_peak, peak)
    fresh = jnp.exp(peak - top)
    new_top = top
    new_total = total * fresh
    new_sum = summed * fresh[..., None]
    top = jnp.maximum(hist_top, new_top)
    old_scale = jnp.exp(hist_top - top)
    new_scale = jnp.exp(new_top - top)
    numer = hist_sum * old_scale[..., None] + new_sum * new_scale[..., None]
    denom = hist_total * old_scale + new_total * new_scale
    return (numer / denom[..., None]).astype(jnp.bfloat16)


def solution(mesh):
    placed = (
        P("groups", "ctx", "head", None),
        P("groups", "ctx", "head", None),
        P("groups", "ctx", "head", None),
        P("groups", "ctx", "head", None),
        P("groups", "ctx", "head", None),
        P("groups", None, "ctx"),
    )
    return jax.shard_map(
        per_device,
        mesh=mesh,
        in_specs=placed,
        out_specs=P("groups", "ctx", "head", None),
        check_vma=False,
    )
```

profile of v0, /device:TPU:22, one launch (start us, length us, event | category | flops | bytes accessed | tf_op | source)
XLA Modules:
  0.0 299.9 jit_solution(13688922537271445588)
XLA Ops:
  8.2 2.8 copy_bitcast_fusion.2
  11.0 47.1 %all-gather.2.cloned.1.call-done = bf16[1,256,32,128]{3,2,0,1:T(8,128)(2,1)} async-done(((bf16[1,32,32,128]{3,2,0,1:T(8,128)(2,1)}), bf16[1,256,32,128]{3,2,0,1:T(8,128)(2,1)}) %all-gather.2.cloned.1.call-update) | async-done | bytes 2097168 | tf_op jit(solution)/shard_map/all_gather | solution.py:51
  58.1 2.4 copy.68
  60.5 52.8 %while.30 = (s32[]{:T(128)}, f32[4,1,8,256]{3,2,1,0:T(8,128)S(1)}, f32[4,1,8,256]{3,2,1,0:T(8,128)S(1)}, f32[4,1,8,256,128]{4,3,2,1,0:T(8,128)}, bf16[4,1,1024,1...) while((s32[]{:T(128)}, f32[4,1,8,256]{3,2,1,0:T(8,128)S(1)}, ...), condition=%wide.region_3.4_spmd.clone, body=%wide.region_0.3_spmd.clone.sunk | while | flops 3783258112 | bytes 28381280 | solution.py:36
  60.6 1.4 fusion.77
  62.0 9.6 %fusion.79 = f32[4,1,8,256,128]{4,3,2,1,0:T(8,128)} fusion(f32[4,1,8,256,128]{4,3,2,1,0:T(8,128)} %get-tuple-element.309, s32[]{:T(128)} %get-tuple-element.306, f32[1024,256,8]{1,0,2:T(8,128)S(1)} %get-tuple-element.281, f32[8,256]{1,0:T(8,128)S(1)} %get-tuple-element.282, pred[256,1024]{0,1:T(8,128)(4,1)S(1)} %bitcast.191, ...), kind=kOutput, calls=%fused_computation.14.clone.1 | convolution fusion | flops 3229614080 | bytes 9970688 | tf_op jit(solution)/shard_map/while/body/eval_jaxpr/sgrc,scd->sgrd/dot_general | solution.py:31
  71.6 2.0 fusion.78
  73.8 1.4 fusion.77
  75.2 9.7 %fusion.79 = f32[4,1,8,256,128]{4,3,2,1,0:T(8,128)} fusion(f32[4,1,8,256,128]{4,3,2,1,0:T(8,128)} %get-tuple-element.309, s32[]{:T(128)} %get-tuple-element.306, f32[1024,256,8]{1,0,2:T(8,128)S(1)} %get-tuple-element.281, f32[8,256]{1,0:T(8,128)S(1)} %get-tuple-element.282, pred[256,1024]{0,1:T(8,128)(4,1)S(1)} %bitcast.191, ...), kind=kOutput, calls=%fused_computation.14.clone.1 | convolution fusion | flops 3229614080 | bytes 9970688 | tf_op jit(solution)/shard_map/while/body/eval_jaxpr/sgrc,scd->sgrd/dot_general | solution.py:31
  84.9 2.0 fusion.78
  87.0 1.4 fusion.77
  88.4 9.7 %fusion.79 = f32[4,1,8,256,128]{4,3,2,1,0:T(8,128)} fusion(f32[4,1,8,256,128]{4,3,2,1,0:T(8,128)} %get-tuple-element.309, s32[]{:T(128)} %get-tuple-element.306, f32[1024,256,8]{1,0,2:T(8,128)S(1)} %get-tuple-element.281, f32[8,256]{1,0:T(8,128)S(1)} %get-tuple-element.282, pred[256,1024]{0,1:T(8,128)(4,1)S(1)} %bitcast.191, ...), kind=kOutput, calls=%fused_computation.14.clone.1 | convolution fusion | flops 3229614080 | bytes 9970688 | tf_op jit(solution)/shard_map/while/body/eval_jaxpr/sgrc,scd->sgrd/dot_general | solution.py:31
  98.1 2.0 fusion.78
  101.6 9.6 %fusion.79 = f32[4,1,8,256,128]{4,3,2,1,0:T(8,128)} fusion(f32[4,1,8,256,128]{4,3,2,1,0:T(8,128)} %get-tuple-element.309, s32[]{:T(128)} %get-tuple-element.306, f32[1024,256,8]{1,0,2:T(8,128)S(1)} %get-tuple-element.281, f32[8,256]{1,0:T(8,128)S(1)} %get-tuple-element.282, pred[256,1024]{0,1:T(8,128)(4,1)S(1)} %bitcast.191, ...), kind=kOutput, calls=%fused_computation.14.clone.1 | convolution fusion | flops 3229614080 | bytes 9970688 | tf_op jit(solution)/shard_map/while/body/eval_jaxpr/sgrc,scd->sgrd/dot_general | solution.py:31
  111.2 2.0 fusion.78
  115.6 5.4 %all-to-all-start.1 = ((f32[8,1,1024]{2,1,0:T(1,128)}), f32[8,1,1024]{2,1,0:T(1,128)S(1)}, u32[]{:S(2)}, u32[]{:S(2)}) async-start(f32[8,1,1024]{2,1,0:T(1,128)} %reshape.378), calls=%async_computation.1 | async-start | bytes 65536 | tf_op jit(solution)/shard_map/all_to_all | solution.py:62
  122.8 1.5 all-to-all-done.1
  124.3 6.7 %all-to-all-start.2 = ((f32[8,1,1024]{2,1,0:T(1,128)}), f32[8,1,1024]{2,1,0:T(1,128)S(1)}, u32[]{:S(2)}, u32[]{:S(2)}) async-start(f32[8,1,1024]{2,1,0:T(1,128)} %reshape.380), calls=%async_computation.2 | async-start | bytes 65536 | tf_op jit(solution)/shard_map/all_to_all | solution.py:63
  131.0 6.6 %copy.67 = f32[1,256,4,8,128]{4,3,2,1,0:T(8,128)} copy(f32[1,256,4,8,128]{4,1,3,0,2:T(8,128)} %bitcast.195) | data formatting | bytes 8388608 | tf_op jit(solution)/shard_map/transpose | solution.py:39
  137.6 6.0 %all-to-all-start = ((f32[1,1,256,32,128]{4,3,1,0,2:T(8,128)}), f32[1,1,256,32,128]{4,3,1,0,2:T(8,128)}, u32[]{:S(2)}, u32[]{:S(2)}) async-start(f32[1,1,256,32,128]{4,3,1,0,2:T(8,128)} %bitcast.193), calls=%async_computation | async-start | bytes 8388608 | tf_op jit(solution)/shard_map/all_to_all | solution.py:64
  143.8 107.1 %all_gather.10 = bf16[1,256,4,128]{3,1,0,2:T(8,128)(2,1)S(1)} all-gather(bf16[1,32,4,128]{3,1,0,2:T(8,128)(2,1)S(1)} %copy.50), channel_id=1, replica_groups=mesh['groups'=2,'ctx'=8,'head'=2] {'ctx'}, dimensions={1}, use_global_device_ids=true | all-gather | bytes 294912 | tf_op jit(solution)/shard_map/all_gather | solution.py:70
  250.9 30.7 %all_gather.11 = bf16[1,256,4,128]{3,1,0,2:T(8,128)(2,1)S(1)} all-gather(bf16[1,32,4,128]{3,1,0,2:T(8,128)(2,1)S(1)} %copy.52), channel_id=1, replica_groups=mesh['groups'=2,'ctx'=8,'head'=2] {'ctx'}, dimensions={1}, use_global_device_ids=true | all-gather | bytes 294912 | tf_op jit(solution)/shard_map/all_gather | solution.py:71
  281.5 3.7 %while.31 = (s32[]{:T(128)}, f32[4,1,8,32]{3,2,1,0:T(8,128)S(1)}, f32[4,1,8,32]{3,2,1,0:T(8,128)S(1)}, f32[4,1,8,32,128]{4,3,2,1,0:T(8,128)S(1)}, bf16[4,1,256,1...) while((s32[]{:T(128)}, f32[4,1,8,32]{3,2,1,0:T(8,128)S(1)}, ...), condition=%wide.region_9.10_spmd.clone, body=%wide.region_6.9_spmd.clone.sunk | while | flops 117972480 | bytes 1172705 | solution.py:36
  287.7 3.9 %fusion.49 = f32[32,32,128]{2,0,1:T(8,128)S(1)} fusion(f32[8,1,32,32,128]{4,3,2,0,1:T(8,128)} %bitcast.8, f32[8,32,32]{1,0,2:T(8,128)S(1)} %copy.48), kind=kLoop, calls=%fused_computation.54 | loop fusion | flops 1966080 | bytes 4751360 | tf_op jit(solution)/shard_map/reduce_sum | solution.py:69
  (72 shorter events, 14.9 us)
Async XLA Ops:
  6.5 51.6 %all-gather.2.cloned.1.call-start = ((), (), s32[]{:S(2)}) async-start(), calls=%async_computation.3 | async-start | bytes 2359296 | tf_op jit(solution)/shard_map/all_gather | solution.py:51
  115.6 8.7 %all-to-all-start.1 = ((f32[8,1,1024]{2,1,0:T(1,128)}), f32[8,1,1024]{2,1,0:T(1,128)S(1)}, u32[]{:S(2)}, u32[]{:S(2)}) async-start(f32[8,1,1024]{2,1,0:T(1,128)} %reshape.378), calls=%async_computation.1 | async-start | bytes 65536 | tf_op jit(solution)/shard_map/all_to_all | solution.py:62
  124.3 13.2 %all-to-all-start.2 = ((f32[8,1,1024]{2,1,0:T(1,128)}), f32[8,1,1024]{2,1,0:T(1,128)S(1)}, u32[]{:S(2)}, u32[]{:S(2)}) async-start(f32[8,1,1024]{2,1,0:T(1,128)} %reshape.380), calls=%async_computation.2 | async-start | bytes 65536 | tf_op jit(solution)/shard_map/all_to_all | solution.py:63
  131.0 12.6 %copy-start = (bf16[1,32,32,128]{3,2,1,0:T(8,128)(2,1)S(1)}, bf16[1,32,32,128]{3,2,1,0:T(8,128)(2,1)}, u32[]{:S(2)}) copy-start(bf16[1,32,32,128]{3,2,1,0:T(8,128)(2,1)} %param.10) | copy-start | bytes 786436
  131.0 12.7 %copy-start.1 = (bf16[1,32,4,128]{3,2,1,0:T(4,128)(2,1)S(1)}, bf16[1,32,4,128]{3,2,1,0:T(4,128)(2,1)}, u32[]{:S(2)}) copy-start(bf16[1,32,4,128]{3,2,1,0:T(4,128)(2,1)} %param.11) | copy-start | bytes 98308
  131.0 12.8 %copy-start.2 = (bf16[1,32,4,128]{3,2,1,0:T(4,128)(2,1)S(1)}, bf16[1,32,4,128]{3,2,1,0:T(4,128)(2,1)}, u32[]{:S(2)}) copy-start(bf16[1,32,4,128]{3,2,1,0:T(4,128)(2,1)} %param.12) | copy-start | bytes 98308
  137.6 150.1 %all-to-all-start = ((f32[1,1,256,32,128]{4,3,1,0,2:T(8,128)}), f32[1,1,256,32,128]{4,3,1,0,2:T(8,128)}, u32[]{:S(2)}, u32[]{:S(2)}) async-start(f32[1,1,256,32,128]{4,3,1,0,2:T(8,128)} %bitcast.193), calls=%async_computation | async-start | bytes 8388608 | tf_op jit(solution)/shard_map/all_to_all | solution.py:64
Sparse Core Ops, SparseCore 0:
  9.5 48.6 all-gather.1
where the time goes:
time: 306 us; the launch traced here: 300 us
  blocking collectives  138 us (45%)
  waiting for transfers between devices  49.4 us (16%)
  matrix products  47.5 us (16%)
  starting transfers between devices  18.1 us (6%)
  other arithmetic  17.1 us (6%)
  local copies, waits for them, and re-layouts  16.1 us (5%)
  between operations  13.6 us (4%)
    all_gather x1, blocking collectives, per_device(): key_piece = lax.all_gather(new_keys, 'ctx', axis=1, tiled=True)  107 us
    all_gather x1, waiting for transfers between devices, per_device(): piece = lax.all_gather(queries, 'ctx', axis=1, tiled=True)  47.1 us
    dot_general x8, matrix products, one_head(): jnp.einsum('sgrc,scd->sgrd', expo, v_head.astype(jnp.float32), precision=...  39.9 us
    all_gather x1, blocking collectives, per_device(): value_piece = lax.all_gather(new_values, 'ctx', axis=1, tiled=True)  30.7 us
    reduce_sum x8, other arithmetic, one_head(): total = jnp.sum(expo, axis=-1)  8.85 us
    dot_general x8, matrix products, one_head(): jnp.einsum('srgd,scd->sgrc', q_head, k_head, preferred_element_type=jnp.f...  6.68 us
    all_to_all x1, starting transfers between devices, per_device(): lax.all_to_all(total_all[None], 'ctx', split_axis=2, concat_axis=0, tiled...  6.65 us
    transpose x1, local copies, waits for them, and re-layouts, attend(): jnp.transpose(summed, (1, 3, 0, 2, 4))  6.58 us
  transfers between devices with their start and end apart: 4, of which 2 were waited for; matrix products, arithmetic and copies ran while one was open for 6% of the time, Pallas kernels for 0%

commit v1 on v0

v1 whole, which is shorter than its diff:
```python
import functools
import math

import jax
import jax.numpy as jnp
from jax import lax
from jax.experimental import pallas as pl
from jax.experimental.pallas import tpu as pltpu
from jax.sharding import PartitionSpec as P

BLK = 128
NEG = -1e30
TINY = 1e-30
TOP = 32767.0
F32 = jnp.float32
BF16 = jnp.bfloat16


def scores_of(q, k):
    return lax.dot_general(q, k, (((1,), (1,)), ((), ())), preferred_element_type=F32)


def weighted(p, v):
    hi = p.astype(BF16)
    lo = (p - hi.astype(F32)).astype(BF16)
    wide = jnp.concatenate([v, jnp.ones_like(v)], axis=1)
    return jnp.dot(hi, wide, preferred_element_type=F32) + jnp.dot(
        lo, wide, preferred_element_type=F32
    )


def compact(x, eye):
    rows = x.shape[0]
    size = eye.shape[0]
    parts = []
    for at in range(0, rows, size):
        piece = jnp.where(eye, x[at : at + size], 0.0)
        parts.append(jnp.sum(piece, axis=0, keepdims=True)[:, :size])
    return parts[0] if len(parts) == 1 else jnp.concatenate(parts, axis=1)


def eye_of(size):
    return lax.broadcasted_iota(jnp.int32, (size, 128), 0) == lax.broadcasted_iota(
        jnp.int32, (size, 128), 1
    )


def hist_kernel(mask_ref, q_ref, k_ref, v_ref, o_ref, st_ref, acc_ref, m_ref):
    chunks, _, rows, hd = q_ref.shape
    b = pl.program_id(1)
    scale = 1.0 / math.sqrt(hd)
    blocks = k_ref.shape[0] // BLK
    acc_ref[...] = jnp.zeros_like(acc_ref)
    m_ref[...] = jnp.full_like(m_ref, NEG)

    @pl.loop(0, blocks)
    def _(j):
        @pl.when(mask_ref[b, j] > 0)
        def _():
            at = pl.ds(pl.multiple_of(j * BLK, BLK), BLK)
            k = k_ref[at, :]
            v = v_ref[at, :]
            for c in range(chunks):
                s = scores_of(q_ref[c, 0], k) * scale
                old = m_ref[c]
                new = jnp.maximum(old, jnp.max(s, axis=1, keepdims=True))
                alpha = jnp.exp(old - new)
                p = jnp.exp(s - new)
                m_ref[c] = new
                acc_ref[c] = acc_ref[c] * jnp.concatenate([alpha, alpha], axis=1) + weighted(p, v)

    eye = eye_of(min(rows, 128))
    for c in range(chunks):
        acc = acc_ref[c]
        num = acc[:, :hd]
        big = jnp.maximum(jnp.max(jnp.abs(num), axis=1, keepdims=True), TINY)
        o_ref[c, 0] = jnp.floor(num * (TOP / big) + 0.5).astype(jnp.int32).astype(jnp.int16)
        st_ref[c, 0, 0:1] = compact(m_ref[c], eye)
        st_ref[c, 0, 1:2] = compact(acc[:, hd:], eye)
        st_ref[c, 0, 2:3] = compact(jnp.broadcast_to(big * (1.0 / TOP), (rows, hd)), eye)
        st_ref[c, 0, 3:8] = jnp.zeros((5, rows), F32)


def new_part(first, q, k, v, group):
    rows, hd = q.shape
    cols = k.shape[0]
    s = scores_of(q, k) * (1.0 / math.sqrt(hd))
    row = first + lax.broadcasted_iota(jnp.int32, (rows, cols), 0) // group
    seen = lax.broadcasted_iota(jnp.int32, (rows, cols), 1) <= row
    s = jnp.where(seen, s, NEG)
    peak = jnp.max(s, axis=1, keepdims=True)
    p = jnp.where(seen, jnp.exp(s - peak), 0.0)
    return jnp.broadcast_to(peak, (rows, hd)), weighted(p, v)


def merged(stats, partial, peak, acc):
    n = len(stats)
    rows, hd = peak.shape
    tops = stats[0][0:1]
    for st in stats[1:]:
        tops = jnp.maximum(tops, st[0:1])
    total = jnp.zeros_like(tops)
    lines = []
    for st in stats:
        w = jnp.exp(st[0:1] - tops)
        total = total + st[1:2] * w
        lines.append(st[2:3] * w)
    lines += [tops, total] + [jnp.zeros_like(tops)] * (-(n + 2) % 8)
    table = jnp.concatenate(lines, axis=0)
    outs = []
    size = min(rows, 128)
    for at in range(0, rows, size):
        cols = jnp.transpose(table[:, at : at + size])
        hist = jnp.zeros((size, hd), F32)
        for d in range(n):
            hist = hist + cols[:, d : d + 1] * partial(d, at, size).astype(jnp.int32).astype(F32)
        mh = cols[:, n : n + 1]
        mn = peak[at : at + size]
        best = jnp.maximum(mh, mn)
        eh = jnp.exp(mh - best)
        en = jnp.exp(mn - best)
        num = eh * hist + en * acc[at : at + size, :hd]
        den = eh * cols[:, n + 1 : n + 2] + en * acc[at : at + size, hd:]
        outs.append(num / den)
    return outs[0] if len(outs) == 1 else jnp.concatenate(outs, axis=0)


def combine_kernel(n, own, q_ref, k_ref, v_ref, o_ref, st_ref, out_ref):
    rows, hd = q_ref.shape[1:]
    first = lax.axis_index("ctx") * own
    peak, acc = new_part(first, q_ref[0], k_ref[...], v_ref[...], rows // own)
    stats = [st_ref[d, 0] for d in range(n)]
    out = merged(stats, lambda d, at, size: o_ref[d, 0, at : at + size], peak, acc)
    out_ref[0] = out.astype(BF16)


def per_device(queries, new_keys, new_values, history_keys, history_values, block_mask):
    _, own, heads, hd = queries.shape
    kv = new_keys.shape[2]
    group = heads // kv
    rows = own * group
    context = history_keys.shape[1]
    n = lax.axis_size("ctx")
    qblocks = block_mask.shape[1]
    chunks = BLK // own

    q = jnp.transpose(queries.reshape(own, kv, group, hd), (1, 0, 2, 3)).reshape(kv, rows, hd)
    q_all = lax.all_gather(q, "ctx", axis=0)
    k_new = lax.all_gather(new_keys.reshape(own, kv * hd), "ctx", axis=0, tiled=True)
    v_new = lax.all_gather(new_values.reshape(own, kv * hd), "ctx", axis=0, tiled=True)
    k_old = history_keys.reshape(context, kv * hd)
    v_old = history_values.reshape(context, kv * hd)

    part, stats = pl.pallas_call(
        hist_kernel,
        grid_spec=pltpu.PrefetchScalarGridSpec(
            num_scalar_prefetch=1,
            grid=(kv, qblocks),
            in_specs=[
                pl.BlockSpec((chunks, 1, rows, hd), lambda g, b, m: (b, g, 0, 0)),
                pl.BlockSpec((context, hd), lambda g, b, m: (0, g)),
                pl.BlockSpec((context, hd), lambda g, b, m: (0, g)),
            ],
            out_specs=[
                pl.BlockSpec((chunks, 1, rows, hd), lambda g, b, m: (b, g, 0, 0)),
                pl.BlockSpec((chunks, 1, 8, rows), lambda g, b, m: (b, g, 0, 0)),
            ],
            scratch_shapes=[
                pltpu.VMEM((chunks, rows, 2 * hd), F32),
                pltpu.VMEM((chunks, rows, hd), F32),
            ],
        ),
        out_shape=[
            jax.ShapeDtypeStruct((n, kv, rows, hd), jnp.int16),
            jax.ShapeDtypeStruct((n, kv, 8, rows), F32),
        ],
        name="hist",
    )(block_mask[0], q_all, k_old, v_old)

    part = lax.all_to_all(part, "ctx", split_axis=0, concat_axis=0, tiled=True)
    stats = lax.all_to_all(stats, "ctx", split_axis=0, concat_axis=0, tiled=True)

    out = pl.pallas_call(
        functools.partial(combine_kernel, n, own),
        grid=(kv,),
        in_specs=[
            pl.BlockSpec((1, rows, hd), lambda g: (g, 0, 0)),
            pl.BlockSpec((n * own, hd), lambda g: (0, g)),
            pl.BlockSpec((n * own, hd), lambda g: (0, g)),
            pl.BlockSpec((n, 1, rows, hd), lambda g: (0, g, 0, 0)),
            pl.BlockSpec((n, 1, 8, rows), lambda g: (0, g, 0, 0)),
        ],
        out_specs=pl.BlockSpec((1, rows, hd), lambda g: (g, 0, 0)),
        out_shape=jax.ShapeDtypeStruct((kv, rows, hd), BF16),
        name="combine",
    )(q, k_new, v_new, part, stats)
    out = jnp.transpose(out.reshape(kv, own, group, hd), (1, 0, 2, 3))
    return out.reshape(1, own, heads, hd)


def solution(mesh):
    spec = P("groups", "ctx", "head", None)
    return jax.shard_map(
        per_device,
        mesh=mesh,
        in_specs=(spec,) * 5 + (P("groups", None, "ctx"),),
        out_specs=spec,
        check_vma=False,
    )
```

time: 306 us -> 221 us (0.72); the launches traced: 300 us -> 218 us
  matrix products: 47.5 us -> 0 us
  Pallas kernels: 0 us -> 18.5 us
  other arithmetic: 17.1 us -> 0 us
  blocking collectives: 138 us -> 124 us
  starting transfers between devices: 18.1 us -> 7.12 us
  local copies, waits for them, and re-layouts: 16.1 us -> 8.06 us
    dot_general x17 -> x0, matrix products: 47.5 us -> none  [the longest x8 39.9 us: one_head(): jnp.einsum('sgrc,scd->sgrd', expo, v_head.astype(jnp.float32), precision=...]
    all_gather x2, blocking collectives: 138 us -> 97.8 us  [the longest x1 65.1 us: per_device(): lax.all_gather(new_values.reshape(own, kv * hd), 'ctx', axis=0, tiled=True)]
    all_to_all x0 -> x1, blocking collectives: none -> 26.7 us  [per_device(): lax.all_to_all(stats, 'ctx', split_axis=0, concat_axis=0, tiled=True)]
    pallas_call x0 -> x2, Pallas kernels: none -> 18.5 us  [the longest x1 12.4 us: per_device(): pl.pallas_call(hist_kernel, grid_spec=pltpu.PrefetchScalarGridSpec(num_sc...]
    reduce_sum x10 -> x0, other arithmetic: 12.9 us -> none  [the longest x8 8.85 us: one_head(): total = jnp.sum(expo, axis=-1)]
    all_to_all x3 -> x1, starting transfers between devices: 18.1 us -> 7.12 us  [per_device(): part = lax.all_to_all(part, 'ctx', split_axis=0, concat_axis=0, tiled=True)]
    transpose x2 -> x0, local copies, waits for them, and re-layouts: 9.38 us -> none  [the longest x1 6.58 us: attend(): jnp.transpose(summed, (1, 3, 0, 2, 4))]
  transfers between devices with their start and end apart: 4 -> 2, of which waited for: 2 -> 1; matrix products, arithmetic and copies ran while one was open for 6% -> 1% of each run, Pallas kernels for 0% -> 0%
where the time goes in v1:
time: 221 us; the launch traced here: 218 us
  blocking collectives  124 us (56%)
  waiting for transfers between devices  46.6 us (21%)
  Pallas kernels  18.5 us (8%)
  between operations  13.4 us (6%)
  local copies, waits for them, and re-layouts  8.06 us (4%)
  starting transfers between devices  7.12 us (3%)
    all_gather x1, blocking collectives, per_device(): lax.all_gather(new_values.reshape(own, kv * hd), 'ctx', axis=0, tiled=True)  65.1 us
    all_gather x1, waiting for transfers between devices, per_device(): q_all = lax.all_gather(q, 'ctx', axis=0)  46.5 us
    all_gather x1, blocking collectives, per_device(): lax.all_gather(new_keys.reshape(own, kv * hd), 'ctx', axis=0, tiled=True)  32.7 us
    all_to_all x1, blocking collectives, per_device(): lax.all_to_all(stats, 'ctx', split_axis=0, concat_axis=0, tiled=True)  26.7 us
    pallas_call x1, Pallas kernels, per_device(): pl.pallas_call(hist_kernel, grid_spec=pltpu.PrefetchScalarGridSpec(num_sc...  12.4 us
    all_to_all x1, starting transfers between devices, per_device(): part = lax.all_to_all(part, 'ctx', split_axis=0, concat_axis=0, tiled=True)  7.12 us
    pallas_call x1, Pallas kernels, per_device(): pl.pallas_call(functools.partial(combine_kernel, n, own), grid=(kv,), in_...  6.05 us
  transfers between devices with their start and end apart: 2, of which 1 were waited for; matrix products, arithmetic and copies ran while one was open for 1% of the time, Pallas kernels for 0%

profile of v1, /device:TPU:22, one launch (start us, length us, event | category | flops | bytes accessed | tf_op | source)
XLA Modules:
  0.0 218.1 jit_solution(5485550086817644732)
XLA Ops:
  6.5 0.0 copy-start
  6.5 0.0 all-gather.2.cloned.1.call-start
  6.5 0.9 copy-done
  7.5 0.8 copy_bitcast_fusion.4
  8.3 0.0 all-gather.2.cloned.1.call-update
  8.4 3.2 %copy_bitcast_fusion = (bf16[1024,512]{1,0:T(8,128)(2,1)}, bf16[1024,512]{1,0:T(8,128)(2,1)}) fusion(bf16[128,8,4,128]{3,2,1,0:T(4,128)(2,1)} %bitcast.36, bf16[128,8,4,128]{3,2,1,0:T(4,128)(2,1)} %bitcast.37), kind=kLoop, calls=%fused_computation | loop fusion | bytes 4194304 | tf_op jit(solution)/shard_map/reshape | solution.py:152
  11.6 46.5 %all-gather.2.cloned.1.call-done.q_ref = bf16[8,4,256,128]{3,2,1,0:T(8,128)(2,1)} async-done(((bf16[1,4,256,128]{3,2,1,0:T(8,128)(2,1)}), bf16[8,4,256,128]{3,2,1,0:T(8,128)(2,1)}) %all-gather.2.cloned.1.call-update) | async-done | bytes 2097168 | tf_op jit(solution)/shard_map/all_gather | solution.py:148
  58.1 12.4 %hist.1 = (s16[8,4,256,128]{3,2,1,0:T(8,128)(2,1)}, f32[8,4,8,256]{3,2,1,0:T(8,128)}) custom-call(s32[2,8]{1,0:T(2,128)} %bitcast.42, bf16[8,4,256,128]{3,2,1,0:T(8,128)(2,1)} %all-gather.2.cloned.1.call-done.q_ref, bf16[1024,512]{1,0:T(8,128)(2,1)} %get-tuple-element.12.k_ref, bf16[1024,512]{1,0:T(8,128)(2,1)} %get-tuple-element.11.v_ref), custom_call_target="tpu_custom_call" | custom-call | tf_op jit(solution)/shard_map/hist/pallas_call | solution.py:154
  70.6 26.7 %all_to_all.10.st_ref = f32[8,4,8,256]{3,2,1,0:T(8,128)} all-to-all(f32[8,4,8,256]{3,2,1,0:T(8,128)} %get-tuple-element.8), channel_id=1, replica_groups=mesh['groups'=2,'ctx'=8,'head'=2] {'ctx'}, dimensions={0} | all-to-all | bytes 524288 | tf_op jit(solution)/shard_map/all_to_all | solution.py:181
  97.2 0.0 copy-start.2
  97.2 0.0 copy-start.3
  97.2 7.1 %all-to-all-start = ((s16[8,4,256,128]{3,2,1,0:T(8,128)(2,1)}), s16[8,4,256,128]{3,2,1,0:T(8,128)(2,1)S(1)}, u32[]{:S(2)}, u32[]{:S(2)}) async-start(s16[8,4,256,128]{3,2,1,0:T(8,128)(2,1)} %get-tuple-element.7), calls=%async_computation | async-start | bytes 4194304 | tf_op jit(solution)/shard_map/all_to_all | solution.py:180
  104.4 0.0 copy-done.2
  104.4 0.0 copy-done.3
  104.4 65.1 %all_gather.10.v_ref = bf16[256,512]{1,0:T(8,128)(2,1)} all-gather(bf16[32,512]{1,0:T(8,128)(2,1)S(1)} %bitcast.39), channel_id=1, replica_groups=mesh['groups'=2,'ctx'=8,'head'=2] {'ctx'}, dimensions={0}, use_global_device_ids=true | all-gather | bytes 294912 | tf_op jit(solution)/shard_map/all_gather | solution.py:150
  169.5 32.7 %all_gather.9.k_ref = bf16[256,512]{1,0:T(8,128)(2,1)} all-gather(bf16[32,512]{1,0:T(8,128)(2,1)S(1)} %bitcast.38), channel_id=1, replica_groups=mesh['groups'=2,'ctx'=8,'head'=2] {'ctx'}, dimensions={0}, use_global_device_ids=true | all-gather | bytes 294912 | tf_op jit(solution)/shard_map/all_gather | solution.py:149
  202.2 0.0 all-to-all-done.o_ref
  202.2 0.0 copy-start.1
  202.2 1.3 copy-done.1
  203.5 6.1 %combine.1 = bf16[4,256,128]{2,1,0:T(8,128)(2,1)} custom-call(bf16[4,256,128]{2,1,0:T(8,128)(2,1)} %get-tuple-element.10.q_ref, bf16[256,512]{1,0:T(8,128)(2,1)} %all_gather.9.k_ref, bf16[256,512]{1,0:T(8,128)(2,1)} %all_gather.10.v_ref, s16[8,4,256,128]{3,2,1,0:T(8,128)(2,1)} %copy-done.1, f32[8,4,8,256]{3,2,1,0:T(8,128)} %all_to_all.10.st_ref), custom_call_target="tpu_custom_call" | custom-call | tf_op jit(solution)/shard_map/combine/pallas_call | solution.py:183
  209.6 1.7 copy_bitcast_fusion.2
  (2 shorter events, 0.0 us)
Async XLA Ops:
  6.5 1.0 copy-start
  6.5 51.6 %all-gather.2.cloned.1.call-start = ((), (), s32[]{:S(2)}) async-start(), calls=%async_computation.2 | async-start | bytes 2359296 | tf_op jit(solution)/shard_map/all_gather | solution.py:148
  97.2 7.1 %copy-start.2 = (bf16[1,32,4,128]{3,2,1,0:T(4,128)(2,1)S(1)}, bf16[1,32,4,128]{3,2,1,0:T(4,128)(2,1)}, u32[]{:S(2)}) copy-start(bf16[1,32,4,128]{3,2,1,0:T(4,128)(2,1)} %param.8) | copy-start | bytes 98308
  97.2 7.1 %copy-start.3 = (bf16[1,32,4,128]{3,2,1,0:T(4,128)(2,1)S(1)}, bf16[1,32,4,128]{3,2,1,0:T(4,128)(2,1)}, u32[]{:S(2)}) copy-start(bf16[1,32,4,128]{3,2,1,0:T(4,128)(2,1)} %param.7) | copy-start | bytes 98308
  97.2 104.9 %all-to-all-start = ((s16[8,4,256,128]{3,2,1,0:T(8,128)(2,1)}), s16[8,4,256,128]{3,2,1,0:T(8,128)(2,1)S(1)}, u32[]{:S(2)}, u32[]{:S(2)}) async-start(s16[8,4,256,128]{3,2,1,0:T(8,128)(2,1)} %get-tuple-element.7), calls=%async_computation | async-start | bytes 4194304 | tf_op jit(solution)/shard_map/all_to_all | solution.py:180
  202.2 1.3 copy-start.1
Sparse Core Ops, SparseCore 0:
  9.5 48.6 all-gather.1

commit v2 on v0

v2 whole, which is shorter than its diff:
```python
import functools
import math

import jax
import jax.numpy as jnp
from jax import lax
from jax.experimental import pallas as pl
from jax.experimental.pallas import tpu as pltpu
from jax.sharding import PartitionSpec as P

BLK = 128
NEG = -1e30
TINY = 1e-30
TOP = 32767.0
F32 = jnp.float32
BF16 = jnp.bfloat16


def scores_of(q, k):
    return lax.dot_general(q, k, (((1,), (1,)), ((), ())), preferred_element_type=F32)


def compact(x, eye):
    rows = x.shape[0]
    size = eye.shape[0]
    parts = []
    for at in range(0, rows, size):
        piece = jnp.where(eye, x[at : at + size], 0.0)
        parts.append(jnp.sum(piece, axis=0, keepdims=True)[:, :size])
    return parts[0] if len(parts) == 1 else jnp.concatenate(parts, axis=1)


def eye_of(size):
    return lax.broadcasted_iota(jnp.int32, (size, 128), 0) == lax.broadcasted_iota(
        jnp.int32, (size, 128), 1
    )


def spread(p, v):
    hi = p.astype(BF16)
    lo = (p - hi.astype(F32)).astype(BF16)
    wide = jnp.concatenate([v, jnp.ones_like(v)], axis=1)
    return jnp.dot(
        jnp.concatenate([hi, lo], axis=1),
        jnp.concatenate([wide, wide], axis=0),
        preferred_element_type=F32,
    )


def fixed(num):
    big = jnp.maximum(jnp.max(jnp.abs(num), axis=1, keepdims=True), TINY)
    coded = jnp.floor(num * (TOP / big) + 0.5).astype(jnp.int32).astype(jnp.int16)
    return coded, jnp.broadcast_to(big * (1.0 / TOP), num.shape)


def remote(src, dst, send, recv, where):
    return pltpu.make_async_remote_copy(
        src_ref=src,
        dst_ref=dst,
        send_sem=send,
        recv_sem=recv,
        device_id={"ctx": where},
        device_id_type=pl.DeviceIdType.MESH,
    )


def places(n):
    far = n // 2
    me = lax.axis_index("ctx")
    z, y = me // 2, me % 2
    order = sorted(range(1, far), key=lambda d: abs(2 * d - far))
    ahead = [((z + d) % far) * 2 for d in range(far)]
    behind = [((z + far - d) % far) * 2 for d in range(far)]
    return far, me, y, order, ahead, behind


def meet(far, y, ahead):
    barrier = pltpu.get_barrier_semaphore()
    for where in [ahead[d] + y for d in range(1, far)] + [ahead[0] + 1 - y]:
        pl.semaphore_signal(
            barrier, inc=1, device_id={"ctx": where}, device_id_type=pl.DeviceIdType.MESH
        )
    pl.semaphore_wait(barrier, far)


def weights_of(stats):
    tops = stats[0][0:1]
    for st in stats[1:]:
        tops = jnp.maximum(tops, st[0:1])
    total = jnp.zeros_like(tops)
    lines = []
    for st in stats:
        w = jnp.exp2(st[0:1] - tops)
        total = total + st[1:2] * w
        lines.append(st[2:3] * w)
    return tops, total, lines


def fused_kernel(
    n, kv, own, mask_ref, q_ref, k_ref, v_ref, kn_ref, vn_ref, out_ref,
    all_ref, s_ref, part_ref, part_st, pair_ref, pair_st, mix_ref, mix_st, line_ref, line_st,
    send_z, recv_z, send_y, recv_y, send_p, recv_p, send_l, recv_l,
):
    far, me, y, order, ahead, behind = places(n)
    rows, hd = q_ref.shape[1:]
    partner = ahead[0] + 1 - y
    z = me // 2
    chunks = BLK // own
    pairs = k_ref.shape[0] // (2 * BLK)
    factor = math.log2(math.e) / math.sqrt(hd)
    eye = eye_of(min(rows, 128))

    meet(far, y, ahead)
    waits = []
    for g in range(kv):
        for d in order:
            waits.append(
                remote(q_ref.at[g], all_ref.at[me, g], send_z.at[d, g], recv_z.at[d, g], ahead[d] + y)
            )
            waits[-1].start()
        waits.append(
            remote(q_ref.at[g], all_ref.at[me, g], send_y.at[0, g], recv_y.at[0, g], partner)
        )
        waits[-1].start()
    all_ref[me] = q_ref[...]

    def relay(g):
        for d in order:
            got = all_ref.at[behind[d] + y, g]
            remote(got, got, send_z.at[d, g], recv_z.at[d, g], ahead[d] + y).wait_recv()
            waits.append(remote(got, got, send_y.at[d, g], recv_y.at[d, g], partner))
            waits[-1].start()

    def arrive(g):
        for d in range(far):
            got = all_ref.at[behind[d] + 1 - y, g]
            remote(got, got, send_y.at[d, g], recv_y.at[d, g], partner).wait_recv()

    def attend(idx, g):
        b = idx // chunks
        q = all_ref[idx, g]
        lanes = slice(g * hd, (g + 1) * hd)
        blank = jnp.zeros((BLK - own, hd), BF16)
        col = lax.broadcasted_iota(jnp.int32, (rows, BLK), 1)
        query = lax.broadcasted_iota(jnp.int32, (rows, BLK), 0) // (rows // own)
        seen = col <= jnp.minimum(query + (idx - me) * own, own - 1)
        s = scores_of(q, jnp.concatenate([kn_ref[:, lanes], blank], axis=0))
        fresh = jnp.where(seen, s * factor, NEG)
        top = fresh
        for t in range(pairs):
            s = scores_of(q, k_ref[t * 2 * BLK : (t + 1) * 2 * BLK, lanes]) * factor
            for half in range(2):
                part = s[:, half * BLK : (half + 1) * BLK]
                part = jnp.where(mask_ref[b, 2 * t + half] > 0, part, NEG)
                s_ref[2 * t + half] = part
                top = jnp.maximum(top, part)
        peak = jnp.maximum(jnp.max(top, axis=1, keepdims=True), 0.5 * NEG)
        acc = spread(
            jnp.exp2(fresh - peak), jnp.concatenate([vn_ref[:, lanes], blank], axis=0)
        )
        for t in range(pairs):
            p = jnp.concatenate(
                [jnp.exp2(s_ref[2 * t] - peak), jnp.exp2(s_ref[2 * t + 1] - peak)], axis=1
            )
            acc = acc + spread(p, v_ref[t * 2 * BLK : (t + 1) * 2 * BLK, lanes])
        coded, step = fixed(acc[:, :hd])
        part_ref[idx, g] = coded
        part_st[idx, g] = jnp.concatenate(
            [
                compact(jnp.broadcast_to(peak, (rows, hd)), eye),
                compact(acc[:, hd:], eye),
                compact(step, eye),
                jnp.zeros((5, rows), F32),
            ],
            axis=0,
        )

    def to_pair(d, g):
        whose = ahead[d] + 1 - y
        return (
            remote(part_st.at[whose, g], pair_st.at[d, g], send_p.at[d, g, 0], recv_p.at[d, g, 0], partner),
            remote(part_ref.at[whose, g], pair_ref.at[d, g], send_p.at[d, g, 1], recv_p.at[d, g, 1], partner),
        )

    def to_line(d, g):
        whose = ahead[d] + y
        return (
            remote(mix_st.at[d, g], line_st.at[d, g], send_l.at[d, g, 0], recv_l.at[d, g, 0], whose),
            remote(mix_ref.at[d, g], line_ref.at[d, g], send_l.at[d, g, 1], recv_l.at[d, g, 1], whose),
        )

    def merge(g):
        for d in order:
            for copy in to_pair(d, g):
                copy.wait_recv()
            whose = ahead[d] + y
            top, total, lines = weights_of([part_st[whose, g], pair_st[d, g]])
            coded, step = fixed(mixed(lines, [part_ref[whose, g], pair_ref[d, g]]))
            mix_ref[d, g] = coded
            mix_st[d, g] = jnp.concatenate(
                [top, total, compact(step, eye), jnp.zeros((5, rows), F32)], axis=0
            )
        for d in order:
            for copy in to_line(d, g):
                copy.start()
                waits.append(copy)

    def finish(g):
        for copy in to_pair(0, g):
            copy.wait_recv()
        for d in order:
            for copy in to_line(d, g):
                copy.wait_recv()
        _, total, lines = weights_of(
            [part_st[me, g], pair_st[0, g]] + [line_st[d, g] for d in order]
        )
        lines = [line / total for line in lines]
        partials = [part_ref[me, g], pair_ref[0, g]] + [line_ref[d, g] for d in order]
        out_ref[g] = mixed(lines, partials).astype(BF16)

    relay(0)
    for g in range(kv):
        arrive(g)

        @pl.loop(0, far)
        def _(t):
            attend(lax.rem(z + t, far) * 2 + 1 - y, g)

        for d in order + [0]:
            for copy in to_pair(d, g):
                copy.start()
                waits.append(copy)
        if g + 1 < kv:
            relay(g + 1)

        @pl.loop(0, far)
        def _(t):
            attend(lax.rem(z + t, far) * 2 + y, g)

        if g > 0:
            merge(g - 1)
        if g > 1:
            finish(g - 2)
    merge(kv - 1)
    for g in range(max(kv - 2, 0), kv):
        finish(g)
    for copy in waits:
        copy.wait_send()


def per_device(queries, new_keys, new_values, history_keys, history_values, block_mask):
    _, own, heads, hd = queries.shape
    kv = new_keys.shape[2]
    group = heads // kv
    rows = own * group
    context = history_keys.shape[1]
    n = lax.axis_size("ctx")
    far = n // 2

    q = jnp.transpose(queries.reshape(own, kv, group, hd), (1, 0, 2, 3)).reshape(kv, rows, hd)
    vmem = pl.BlockSpec(memory_space=pltpu.VMEM)
    dma = pltpu.SemaphoreType.DMA
    slots = [
        pltpu.VMEM((far, kv, rows, hd), jnp.int16),
        pltpu.VMEM((far, kv, 8, rows), F32),
    ]
    out = pl.pallas_call(
        functools.partial(fused_kernel, n, kv, own),
        in_specs=[pl.BlockSpec(memory_space=pltpu.SMEM)] + [vmem] * 5,
        out_specs=vmem,
        out_shape=jax.ShapeDtypeStruct((kv, rows, hd), BF16),
        scratch_shapes=[
            pltpu.VMEM((n, kv, rows, hd), BF16),
            pltpu.VMEM((context // BLK, rows, BLK), F32),
            pltpu.VMEM((n, kv, rows, hd), jnp.int16),
            pltpu.VMEM((n, kv, 8, rows), F32),
        ]
        + slots * 3
        + [dma((far, kv))] * 4
        + [dma((far, kv, 2))] * 4,
        compiler_params=pltpu.CompilerParams(collective_id=0, has_side_effects=True),
        name="fused",
    )(
        block_mask[0],
        q,
        history_keys.reshape(context, kv * hd),
        history_values.reshape(context, kv * hd),
        new_keys.reshape(own, kv * hd),
        new_values.reshape(own, kv * hd),
    )
    out = jnp.transpose(out.reshape(kv, own, group, hd), (1, 0, 2, 3))
    return out.reshape(1, own, heads, hd)


def mixed(lines, partials):
    rows, hd = partials[0].shape
    size = min(rows, 128)
    table = jnp.concatenate(
        lines + [jnp.zeros_like(lines[0])] * (-len(lines) % 8), axis=0
    )
    outs = []
    for at in range(0, rows, size):
        cols = jnp.transpose(table[:, at : at + size])
        total = jnp.zeros((size, hd), F32)
        for i, part in enumerate(partials):
            total = total + cols[:, i : i + 1] * part[at : at + size].astype(jnp.int32).astype(F32)
        outs.append(total)
    return outs[0] if len(outs) == 1 else jnp.concatenate(outs, axis=0)


def solution(mesh):
    spec = P("groups", "ctx", "head", None)
    return jax.shard_map(
        per_device,
        mesh=mesh,
        in_specs=(spec,) * 5 + (P("groups", None, "ctx"),),
        out_specs=spec,
        check_vma=False,
    )
```

time: 306 us -> 93.4 us (0.31); the launches traced: 300 us -> 93.1 us
  blocking collectives: 138 us -> 0 us
  Pallas kernels: 0 us -> 86 us
  waiting for transfers between devices: 49.4 us -> 0 us
  matrix products: 47.5 us -> 0 us
  starting transfers between devices: 18.1 us -> 0 us
  other arithmetic: 17.1 us -> 0 us
  between operations: 13.6 us -> 0.01 us
  local copies, waits for them, and re-layouts: 16.1 us -> 7.12 us
    all_gather x2 -> x0, blocking collectives: 138 us -> none  [the longest x1 107 us: per_device(): key_piece = lax.all_gather(new_keys, 'ctx', axis=1, tiled=True)]
    pallas_call x0 -> x1, Pallas kernels: none -> 86 us  [per_device(): pl.pallas_call(functools.partial(fused_kernel, n, kv, own), in_specs=[pl....]
    dot_general x17 -> x0, matrix products: 47.5 us -> none  [the longest x8 39.9 us: one_head(): jnp.einsum('sgrc,scd->sgrd', expo, v_head.astype(jnp.float32), precision=...]
    all_gather x1 -> x0, waiting for transfers between devices: 47.1 us -> none  [per_device(): piece = lax.all_gather(queries, 'ctx', axis=1, tiled=True)]
    all_to_all x3 -> x0, starting transfers between devices: 18.1 us -> none  [the longest x1 6.65 us: per_device(): lax.all_to_all(total_all[None], 'ctx', split_axis=2, concat_axis=0, tiled...]
    reduce_sum x10 -> x0, other arithmetic: 12.9 us -> none  [the longest x8 8.85 us: one_head(): total = jnp.sum(expo, axis=-1)]
    transpose x2 -> x0, local copies, waits for them, and re-layouts: 9.38 us -> none  [the longest x1 6.58 us: attend(): jnp.transpose(summed, (1, 3, 0, 2, 4))]
    reshape x1 -> x4, local copies, waits for them, and re-layouts: 2.4 us -> 7.11 us  [the longest x1 3.22 us: per_device(): history_values.reshape(context, kv * hd)]
  transfers between devices with their start and end apart: 4 -> 0, of which waited for: 2 -> 0; matrix products, arithmetic and copies ran while one was open for 6% -> 0% of each run, Pallas kernels for 0% -> 0%
where the time goes in v2:
time: 93.4 us; the launch traced here: 93.1 us
  Pallas kernels  86 us (92%)
  local copies, waits for them, and re-layouts  7.12 us (8%)
    pallas_call x1, Pallas kernels, per_device(): pl.pallas_call(functools.partial(fused_kernel, n, kv, own), in_specs=[pl....  86 us
    reshape x1, local copies, waits for them, and re-layouts, per_device(): history_values.reshape(context, kv * hd)  3.22 us

profile of v2, /device:TPU:22, one launch (start us, length us, event | category | flops | bytes accessed | tf_op | source)
XLA Modules:
  0.0 93.1 jit_solution(1151886231282350842)
XLA Ops:
  0.0 0.0 copy-start
  0.0 1.4 %copy_bitcast_fusion.4 = (bf16[32,512]{1,0:T(8,128)(2,1)}, bf16[32,512]{1,0:T(8,128)(2,1)}) fusion(bf16[4,8,4,128]{3,2,1,0:T(4,128)(2,1)} %bitcast.33, bf16[4,8,4,128]{3,2,1,0:T(4,128)(2,1)} %bitcast.34), kind=kLoop, calls=%fused_computation.4 | loop fusion | bytes 131072 | tf_op jit(solution)/shard_map/reshape | solution.py:289
  1.5 0.0 copy-done
  1.5 0.7 copy_bitcast_fusion.3.q_ref
  2.2 3.2 %copy_bitcast_fusion = (bf16[1024,512]{1,0:T(8,128)(2,1)}, bf16[1024,512]{1,0:T(8,128)(2,1)}) fusion(bf16[128,8,4,128]{3,2,1,0:T(4,128)(2,1)} %bitcast.31, bf16[128,8,4,128]{3,2,1,0:T(4,128)(2,1)} %bitcast.32), kind=kLoop, calls=%fused_computation | loop fusion | bytes 4194304 | tf_op jit(solution)/shard_map/reshape | solution.py:287
  5.4 86.0 %fused.1 = bf16[4,256,128]{2,1,0:T(8,128)(2,1)} custom-call(s32[2,8]{1,0:T(2,128)} %bitcast.35, bf16[4,256,128]{2,1,0:T(8,128)(2,1)} %copy_bitcast_fusion.3.q_ref, bf16[1024,512]{1,0:T(8,128)(2,1)} %get-tuple-element.6.k_ref, bf16[1024,512]{1,0:T(8,128)(2,1)} %get-tuple-element.5.v_ref, bf16[32,512]{1,0:T(8,128)(2,1)} %get-tuple-element.8.kn_ref, ...), custom_call_target="tpu_custom_call" | custom-call | tf_op jit(solution)/shard_map/fused/pallas_call | solution.py:267
  91.4 1.7 %copy_bitcast_fusion.2 = bf16[1,32,32,128]{3,2,1,0:T(8,128)(2,1)} fusion(bf16[4,256,128]{2,1,0:T(8,128)(2,1)} %fused.1), kind=kLoop, calls=%fused_computation.2 | loop fusion | bytes 524288 | tf_op jit(solution)/shard_map/reshape | solution.py:292
Async XLA Ops:
  0.0 1.5 %copy-start = (bf16[1,32,32,128]{3,2,1,0:T(8,128)(2,1)S(1)}, bf16[1,32,32,128]{3,2,1,0:T(8,128)(2,1)}, u32[]{:S(2)}) copy-start(bf16[1,32,32,128]{3,2,1,0:T(8,128)(2,1)} %param.6) | copy-start | bytes 786436

commit v3 on v2

--- a/solution.py
+++ b/solution.py
@@ -33,17 +33,6 @@
 def eye_of(size):
     return lax.broadcasted_iota(jnp.int32, (size, 128), 0) == lax.broadcasted_iota(
         jnp.int32, (size, 128), 1
-    )
-
-
-def spread(p, v):
-    hi = p.astype(BF16)
-    lo = (p - hi.astype(F32)).astype(BF16)
-    wide = jnp.concatenate([v, jnp.ones_like(v)], axis=1)
-    return jnp.dot(
-        jnp.concatenate([hi, lo], axis=1),
-        jnp.concatenate([wide, wide], axis=0),
-        preferred_element_type=F32,
     )
 
 
@@ -98,7 +87,7 @@
 
 def fused_kernel(
     n, kv, own, mask_ref, q_ref, k_ref, v_ref, kn_ref, vn_ref, out_ref,
-    all_ref, s_ref, part_ref, part_st, pair_ref, pair_st, mix_ref, mix_st, line_ref, line_st,
+    all_ref, s_ref, p_ref, wide_ref, part_ref, part_st, pair_ref, pair_st, mix_ref, mix_st, line_ref, line_st,
     send_z, recv_z, send_y, recv_y, send_p, recv_p, send_l, recv_l,
 ):
     far, me, y, order, ahead, behind = places(n)
@@ -136,44 +125,84 @@
             got = all_ref.at[behind[d] + 1 - y, g]
             remote(got, got, send_y.at[d, g], recv_y.at[d, g], partner).wait_recv()
 
-    def attend(idx, g):
-        b = idx // chunks
-        q = all_ref[idx, g]
+    def widen(g):
+        lanes = slice(g * hd, (g + 1) * hd)
+        blank = jnp.zeros((BLK - own, hd), BF16)
+        ones = jnp.ones((2 * BLK, hd), BF16)
+        fresh = jnp.concatenate([vn_ref[:, lanes], blank], axis=0)
+        wide_ref[: 2 * BLK, :hd] = jnp.concatenate([fresh, fresh], axis=0)
+        wide_ref[: 2 * BLK, hd:] = ones
+        for t in range(pairs):
+            v = v_ref[t * 2 * BLK : (t + 1) * 2 * BLK, lanes]
+            for copy in range(2):
+                at = 2 * BLK * (1 + 2 * t + copy)
+                wide_ref[at : at + 2 * BLK, :hd] = v
+                wide_ref[at : at + 2 * BLK, hd:] = ones
+
+    def split(at, p):
+        cols = p.shape[1]
+        hi = p.astype(BF16)
+        p_ref[:, at : at + cols] = hi
+        p_ref[:, at + cols : at + 2 * cols] = (p - hi.astype(F32)).astype(BF16)
+
+    def attend(both, g):
+        q = jnp.concatenate([all_ref[idx, g] for idx in both], axis=0)
         lanes = slice(g * hd, (g + 1) * hd)
         blank = jnp.zeros((BLK - own, hd), BF16)
         col = lax.broadcasted_iota(jnp.int32, (rows, BLK), 1)
         query = lax.broadcasted_iota(jnp.int32, (rows, BLK), 0) // (rows // own)
-        seen = col <= jnp.minimum(query + (idx - me) * own, own - 1)
-        s = scores_of(q, jnp.concatenate([kn_ref[:, lanes], blank], axis=0))
-        fresh = jnp.where(seen, s * factor, NEG)
+        s = scores_of(q, jnp.concatenate([kn_ref[:, lanes], blank], axis=0)) * factor
+        fresh = jnp.concatenate(
+            [
+                jnp.where(
+                    col <= jnp.minimum(query + (idx - me) * own, own - 1),
+                    s[i * rows : (i + 1) * rows],
+                    NEG,
+                )
+                for i, idx in enumerate(both)
+            ],
+            axis=0,
+        )
         top = fresh
         for t in range(pairs):
             s = scores_of(q, k_ref[t * 2 * BLK : (t + 1) * 2 * BLK, lanes]) * factor
             for half in range(2):
                 part = s[:, half * BLK : (half + 1) * BLK]
-                part = jnp.where(mask_ref[b, 2 * t + half] > 0, part, NEG)
+                part = jnp.concatenate(
+                    [
+                        jnp.where(
+                            mask_ref[idx // chunks, 2 * t + half] > 0,
+                            part[i * rows : (i + 1) * rows],
+                            NEG,
+                        )
+                        for i, idx in enumerate(both)
+                    ],
+                    axis=0,
+                )
                 s_ref[2 * t + half] = part
                 top = jnp.maximum(top, part)
         peak = jnp.maximum(jnp.max(top, axis=1, keepdims=True), 0.5 * NEG)
-        acc = spread(
-            jnp.exp2(fresh - peak), jnp.concatenate([vn_ref[:, lanes], blank], axis=0)
-        )
+        split(0, jnp.exp2(fresh - peak))
         for t in range(pairs):
             p = jnp.concatenate(
                 [jnp.exp2(s_ref[2 * t] - peak), jnp.exp2(s_ref[2 * t + 1] - peak)], axis=1
             )
-            acc = acc + spread(p, v_ref[t * 2 * BLK : (t + 1) * 2 * BLK, lanes])
+            split(2 * BLK * (1 + 2 * t), p)
+        acc = jnp.dot(p_ref[...], wide_ref[...], preferred_element_type=F32)
         coded, step = fixed(acc[:, :hd])
-        part_ref[idx, g] = coded
-        part_st[idx, g] = jnp.concatenate(
-            [
-                compact(jnp.broadcast_to(peak, (rows, hd)), eye),
-                compact(acc[:, hd:], eye),
-                compact(step, eye),
-                jnp.zeros((5, rows), F32),
-            ],
-            axis=0,
-        )
+        peak = jnp.broadcast_to(peak, coded.shape)
+        for i, idx in enumerate(both):
+            at = slice(i * rows, (i + 1) * rows)
+            part_ref[idx, g] = coded[at]
+            part_st[idx, g] = jnp.concatenate(
+                [
+                    compact(peak[at], eye),
+                    compact(acc[at, hd:], eye),
+                    compact(step[at], eye),
+                    jnp.zeros((5, rows), F32),
+                ],
+                axis=0,
+            )
 
     def to_pair(d, g):
         whose = ahead[d] + 1 - y
@@ -220,11 +249,12 @@
 
     relay(0)
     for g in range(kv):
+        widen(g)
         arrive(g)
 
-        @pl.loop(0, far)
+        @pl.loop(0, far // 2)
         def _(t):
-            attend(lax.rem(z + t, far) * 2 + 1 - y, g)
+            attend([lax.rem(z + 2 * t + i, far) * 2 + 1 - y for i in range(2)], g)
 
         for d in order + [0]:
             for copy in to_pair(d, g):
@@ -233,9 +263,9 @@
         if g + 1 < kv:
             relay(g + 1)
 
-        @pl.loop(0, far)
+        @pl.loop(0, far // 2)
         def _(t):
-            attend(lax.rem(z + t, far) * 2 + y, g)
+            attend([lax.rem(z + 2 * t + i, far) * 2 + y for i in range(2)], g)
 
         if g > 0:
             merge(g - 1)
@@ -271,7 +301,9 @@
         out_shape=jax.ShapeDtypeStruct((kv, rows, hd), BF16),
         scratch_shapes=[
             pltpu.VMEM((n, kv, rows, hd), BF16),
-            pltpu.VMEM((context // BLK, rows, BLK), F32),
+            pltpu.VMEM((context // BLK, 2 * rows, BLK), F32),
+            pltpu.VMEM((2 * rows, 2 * (context + BLK)), BF16),
+            pltpu.VMEM((2 * (context + BLK), 2 * hd), BF16),
             pltpu.VMEM((n, kv, rows, hd), jnp.int16),
             pltpu.VMEM((n, kv, 8, rows), F32),
         ]

time: 93.4 us -> 90.1 us (0.965)
  Pallas kernels: 86 us -> 82.7 us
    pallas_call x1, Pallas kernels: 86 us -> 82.7 us  [per_device(): pl.pallas_call(functools.partial(fused_kernel, n, kv, own), in_specs=[pl....]
where the time goes in v3:
time: 90.1 us; the launch traced here: 89.9 us
  Pallas kernels  82.7 us (92%)
  local copies, waits for them, and re-layouts  7.12 us (8%)
    pallas_call x1, Pallas kernels, per_device(): pl.pallas_call(functools.partial(fused_kernel, n, kv, own), in_specs=[pl....  82.7 us
    reshape x1, local copies, waits for them, and re-layouts, per_device(): history_values.reshape(context, kv * hd)  3.22 us

profile of v3, /device:TPU:22, one launch (start us, length us, event | category | flops | bytes accessed | tf_op | source)
XLA Modules:
  0.0 89.9 jit_solution(5801567517070155226)
XLA Ops:
  0.0 0.0 copy-start
  0.0 1.4 %copy_bitcast_fusion.4 = (bf16[32,512]{1,0:T(8,128)(2,1)}, bf16[32,512]{1,0:T(8,128)(2,1)}) fusion(bf16[4,8,4,128]{3,2,1,0:T(4,128)(2,1)} %bitcast.33, bf16[4,8,4,128]{3,2,1,0:T(4,128)(2,1)} %bitcast.34), kind=kLoop, calls=%fused_computation.4 | loop fusion | bytes 131072 | tf_op jit(solution)/shard_map/reshape | solution.py:321
  1.5 0.0 copy-done
  1.5 0.7 copy_bitcast_fusion.3.q_ref
  2.2 3.2 %copy_bitcast_fusion = (bf16[1024,512]{1,0:T(8,128)(2,1)}, bf16[1024,512]{1,0:T(8,128)(2,1)}) fusion(bf16[128,8,4,128]{3,2,1,0:T(4,128)(2,1)} %bitcast.31, bf16[128,8,4,128]{3,2,1,0:T(4,128)(2,1)} %bitcast.32), kind=kLoop, calls=%fused_computation | loop fusion | bytes 4194304 | tf_op jit(solution)/shard_map/reshape | solution.py:319
  5.4 82.7 %fused.1 = bf16[4,256,128]{2,1,0:T(8,128)(2,1)} custom-call(s32[2,8]{1,0:T(2,128)} %bitcast.35, bf16[4,256,128]{2,1,0:T(8,128)(2,1)} %copy_bitcast_fusion.3.q_ref, bf16[1024,512]{1,0:T(8,128)(2,1)} %get-tuple-element.6.k_ref, bf16[1024,512]{1,0:T(8,128)(2,1)} %get-tuple-element.5.v_ref, bf16[32,512]{1,0:T(8,128)(2,1)} %get-tuple-element.8.kn_ref, ...), custom_call_target="tpu_custom_call" | custom-call | tf_op jit(solution)/shard_map/fused/pallas_call | solution.py:297
  88.2 1.7 %copy_bitcast_fusion.2 = bf16[1,32,32,128]{3,2,1,0:T(8,128)(2,1)} fusion(bf16[4,256,128]{2,1,0:T(8,128)(2,1)} %fused.1), kind=kLoop, calls=%fused_computation.2 | loop fusion | bytes 524288 | tf_op jit(solution)/shard_map/reshape | solution.py:324
Async XLA Ops:
  0.0 1.5 %copy-start = (bf16[1,32,32,128]{3,2,1,0:T(8,128)(2,1)S(1)}, bf16[1,32,32,128]{3,2,1,0:T(8,128)(2,1)}, u32[]{:S(2)}) copy-start(bf16[1,32,32,128]{3,2,1,0:T(8,128)(2,1)} %param.6) | copy-start | bytes 786436
